TPU v7x, 512 devices: a whole 4x8x8 slice. The times are simulated.
512 devices in a mesh: row: 16 (over y_lo, x, core), col: 32 (over y_hi, z).
Axes of the slice: x: 4, y: 8 (y_hi: 4, y_lo: 2; y = y_hi * 2 + y_lo), z: 8, core: 2. Of those that a mesh axis runs over, the one named last changes fastest.
Arguments:
- vectors: float32 [2048, 16384], P('row', 'col'), may hold values from -6 to 6
- factors: float32 [32, 4, 512, 512], P('col', None, 'row'), may hold values from -1 to 1, as said below
- offsets: int32 [32], replicated, may hold values from 0 to 1
Outputs:
- updated: float32 [2048, 16384], P('row', 'col')
Inputs may be any that keep to these rules, and one draw needn't show every extreme that they name: Each factors[c, k] is an orthogonal matrix.
All inputs are finite; a program needn't handle non-finite values.
Results may differ from a plain program's by a relative error of at most 0.00014.
Values sent between devices are 32-bit elements; how exact they have to be, the bound alone decides.
A program may use at most 64 MiB of HBM per device.

v0:
```python
import jax
import jax.numpy as jnp
from jax import lax
from jax.sharding import PartitionSpec as P


def passed_along(block, axis, distance):
    devices = range(lax.axis_size(axis))
    route = [(i - distance, i) for i in devices if i - distance in devices]
    return lax.ppermute(block, axis, route)


def product(former, latter):
    return jnp.dot(
        former, latter, precision=lax.Precision.HIGHEST, preferred_element_type=jnp.float32
    )


def one_by_one(section, factor_list, stride):
    for factor_no in range(4):
        before = section[:, : factor_no * stride]
        middle = section[:, factor_no * stride : factor_no * stride + 2 * stride]
        beyond = section[:, factor_no * stride + 2 * stride :]
        section = jnp.concatenate([before, product(middle, factor_list[factor_no]), beyond], 1)
    return section


def keep_panel(assembled):
    return assembled


def on_device(vectors, factors, offsets):
    block_cols = vectors.shape[1]
    stride = block_cols // 2
    column = lax.axis_index("col")
    groups = lax.axis_size("col")
    gathered = lax.all_gather(factors, "row", axis=2, tiled=True)
    chain_factors = gathered[0]
    offset = lax.dynamic_index_in_dim(offsets, column, 0, keepdims=False)
    first_col = offset * stride
    identity = jnp.eye(2 * stride, dtype=jnp.float32)
    global_first = column * block_cols + first_col
    factor_list = []
    for factor_no in range(4):
        valid = global_first + factor_no * stride + 2 * stride <= groups * block_cols
        factor_list.append(jnp.where(valid, chain_factors[factor_no], identity))

    def update(assembled):
        section = lax.dynamic_slice_in_dim(assembled, first_col, 5 * stride, 1)
        section = one_by_one(section, factor_list, stride)
        return lax.dynamic_update_slice_in_dim(assembled, section, first_col, 1)

    current = vectors
    for tick_num in range(3):
        position = jnp.mod(column - tick_num, 3)
        leader = column - position
        active = leader >= 0
        beside = passed_along(current, "col", -1)
        distant = passed_along(current, "col", -2)
        assembled = jnp.concatenate([current, beside, distant], 1)
        changed = lax.cond(active & (position == 0), update, keep_panel, assembled)
        back_near = passed_along(changed[:, block_cols : 2 * block_cols], "col", 1)
        back_far = passed_along(changed[:, 2 * block_cols :], "col", 2)
        chosen = jnp.where(
            position == 0, changed[:, :block_cols], jnp.where(position == 1, back_near, back_far)
        )
        current = jnp.where(active, chosen, current)
    return current


def solution(mesh):
    placed = (P("row", "col"), P("col", None, "row", None), P())
    return jax.shard_map(
        on_device, mesh=mesh, in_specs=placed, out_specs=P("row", "col"), check_vma=False
    )
```

profile of v0, /device:TPU:112, one launch (start us, length us, event | category | flops | bytes accessed | tf_op | source)
XLA Modules:
  0.0 247.6 jit_solution(17116468013829115699)
XLA Ops:
  7.3 1.9 collective-permute-start
  9.2 12.2 %collective-permute-start.1 = (f32[128,512]{1,0:T(8,128)}, f32[128,512]{1,0:T(8,128)S(1)}, u32[]{:S(2)}, u32[]{:S(2)}) collective-permute-start(f32[128,512]{1,0:T(8,128)} %param.9), channel_id=1, source_target_pairs={{2,0},{3,1},{4,2},{5,3},{6,4},{7,5},{8,6},{9,7},{10,8},{11,9},{12,... | collective-permute-start | bytes 786440 | tf_op jit(solution)/shard_map/ppermute | solution.py:10
  24.3 8.9 %collective-permute-done.1 = f32[128,512]{1,0:T(8,128)S(1)} collective-permute-done((f32[128,512]{1,0:T(8,128)}, f32[128,512]{1,0:T(8,128)S(1)}, u32[]{:S(2)}, u32[]{:S(2)}) %collective-permute-start.1) | collective-permute-done | bytes 262176 | tf_op jit(solution)/shard_map/ppermute | solution.py:10
  34.1 21.1 %all-gather.2.cloned.1.call-done = f32[1,4,512,512]{3,2,1,0:T(8,128)} async-done(((f32[1,4,32,512]{3,2,1,0:T(8,128)}), f32[1,4,512,512]{3,2,1,0:T(8,128)}) %all-gather.2.cloned.1.call-update) | async-done | bytes 4194320 | tf_op jit(solution)/shard_map/all_gather | solution.py:37
  55.2 3.7 %convert_select_fusion = (f32[512,512]{1,0:T(8,128)S(1)}, f32[512,512]{1,0:T(8,128)S(1)}, f32[512,512]{1,0:T(8,128)}, f32[512,512]{1,0:T(8,128)S(1)}) fusion(f32[1,4,512,512]{3,2,1,0:T(8,128)} %all-gather.2.cloned.1.call-done, pred[]{:T(512)S(6)} %le.15, pred[]{:T(512)S(6)} %le.14, pred[]{:T(512)S(6)} %le.13, pred[]{:T(512)S(6)} %le.12), kind=kLoop, calls=%fused_computation.69 | loop fusion | flops 1572864 | bytes 8388612 | tf_op jit(solution)/shard_map/jit(_where)/select_n | solution.py:46
  60.8 3.5 %collective-permute-start.2 = (f32[128,512]{1,0:T(8,128)}, f32[128,512]{1,0:T(8,128)S(1)}, u32[]{:S(2)}, u32[]{:S(2)}) collective-permute-start(f32[128,512]{1,0:T(8,128)} %get-tuple-element.80), channel_id=1, source_target_pairs={{0,1},{1,2},{2,3},{3,4},{4,5},{5,6},{6,7},{7,8},{8,9},{9,10},{10,1... | collective-permute-start | bytes 786440 | tf_op jit(solution)/shard_map/ppermute | solution.py:10
  64.3 20.9 %collective-permute-start.3 = (f32[128,512]{1,0:T(8,128)}, f32[128,512]{1,0:T(8,128)}, u32[]{:S(2)}, u32[]{:S(2)}) collective-permute-start(f32[128,512]{1,0:T(8,128)} %get-tuple-element.79), channel_id=1, source_target_pairs={{0,2},{1,3},{2,4},{3,5},{4,6},{5,7},{6,8},{7,9},{8,10},{9,11},{10,... | collective-permute-start | bytes 786440 | tf_op jit(solution)/shard_map/ppermute | solution.py:10
  85.3 5.4 %collective-permute-done.2 = f32[128,512]{1,0:T(8,128)S(1)} collective-permute-done((f32[128,512]{1,0:T(8,128)}, f32[128,512]{1,0:T(8,128)S(1)}, u32[]{:S(2)}, u32[]{:S(2)}) %collective-permute-start.2) | collective-permute-done | bytes 262176 | tf_op jit(solution)/shard_map/ppermute | solution.py:10
  91.3 19.8 %collective-permute-done.3 = f32[128,512]{1,0:T(8,128)} collective-permute-done((f32[128,512]{1,0:T(8,128)}, f32[128,512]{1,0:T(8,128)}, u32[]{:S(2)}, u32[]{:S(2)}) %collective-permute-start.3) | collective-permute-done | bytes 262176 | tf_op jit(solution)/shard_map/ppermute | solution.py:10
  112.3 1.9 collective-permute-start.4
  114.2 1.9 collective-permute-start.5
  116.2 9.7 %collective-permute-done.4 = f32[128,512]{1,0:T(8,128)} collective-permute-done((f32[128,512]{1,0:T(8,128)S(1)}, f32[128,512]{1,0:T(8,128)}, u32[]{:S(2)}, u32[]{:S(2)}) %collective-permute-start.4) | collective-permute-done | bytes 262176 | tf_op jit(solution)/shard_map/ppermute | solution.py:10
  125.9 5.3 %collective-permute-done.5 = f32[128,512]{1,0:T(8,128)} collective-permute-done((f32[128,512]{1,0:T(8,128)S(1)}, f32[128,512]{1,0:T(8,128)}, u32[]{:S(2)}, u32[]{:S(2)}) %collective-permute-start.5) | collective-permute-done | bytes 262176 | tf_op jit(solution)/shard_map/ppermute | solution.py:10
  131.2 2.0 pad_maximum_fusion.27
  133.1 18.0 %conditional.4 = (f32[128,1536]{1,0:T(8,128)}) conditional(s32[]{:T(128)} %convert_element_type.19, f32[128,1536]{1,0:T(8,128)} %pad_maximum_fusion.27, (s32[]{:T(128)}, f32[128,1536]{1,0:T(8,128)}, f32[512,512]{1,0:T(8,128)S(1)}, f32[512,512]{1,0:T(8,128)}, f32[512,512]{1,0:T(8,128)S(1)}, /*index=5*/f32[512,512]{1,0:T(8,128)S(1)}) %tuple.24), branch_computations={%region_2.3_spmd, %region_3.4_spmd} | conditional | flops 1611464704 | bytes 13762710 | solution.py:61
  133.1 2.4 fusion.18
  136.8 2.0 fusion.16
  144.8 1.9 pad_maximum_fusion.9
  146.7 4.4 %dynamic_update_slice.7 = f32[128,1536]{1,0:T(8,128)} dynamic-update-slice(f32[128,1536]{1,0:T(8,128)} %get-tuple-element.59, f32[128,1280]{1,0:T(8,128)} %pad_maximum_fusion.9, s32[]{:T(128)} %constant.40.clone, s32[]{:T(128)S(6)} %select_n.81) | dynamic-update-slice | bytes 1310724 | tf_op jit(solution)/shard_map/cond/branch_1_fun/dynamic_update_slice | solution.py:51
  153.0 1.9 collective-permute-start.6
  154.9 1.9 collective-permute-start.7
  156.8 9.2 %collective-permute-done.6 = f32[128,512]{1,0:T(8,128)S(1)} collective-permute-done((f32[128,512]{1,0:T(8,128)}, f32[128,512]{1,0:T(8,128)S(1)}, u32[]{:S(2)}, u32[]{:S(2)}) %collective-permute-start.6) | collective-permute-done | bytes 262176 | tf_op jit(solution)/shard_map/ppermute | solution.py:10
  166.8 9.5 %collective-permute-done.7 = f32[128,512]{1,0:T(8,128)} collective-permute-done((f32[128,512]{1,0:T(8,128)}, f32[128,512]{1,0:T(8,128)}, u32[]{:S(2)}, u32[]{:S(2)}) %collective-permute-start.7) | collective-permute-done | bytes 262176 | tf_op jit(solution)/shard_map/ppermute | solution.py:10
  177.3 2.2 collective-permute-start.8
  179.5 8.8 %collective-permute-start.9 = (f32[128,512]{1,0:T(8,128)S(1)}, f32[128,512]{1,0:T(8,128)}, u32[]{:S(2)}, u32[]{:S(2)}) collective-permute-start(f32[128,512]{1,0:T(8,128)S(1)} %fusion.37), channel_id=1, source_target_pairs={{2,0},{3,1},{4,2},{5,3},{6,4},{7,5},{8,6},{9,7},{10,8},{11,9},{12,... | collective-permute-start | bytes 786440 | tf_op jit(solution)/shard_map/ppermute | solution.py:10
  188.3 3.4 %collective-permute-done.8 = f32[128,512]{1,0:T(8,128)} collective-permute-done((f32[128,512]{1,0:T(8,128)S(1)}, f32[128,512]{1,0:T(8,128)}, u32[]{:S(2)}, u32[]{:S(2)}) %collective-permute-start.8) | collective-permute-done | bytes 262176 | tf_op jit(solution)/shard_map/ppermute | solution.py:10
  191.7 3.9 %collective-permute-done.9 = f32[128,512]{1,0:T(8,128)} collective-permute-done((f32[128,512]{1,0:T(8,128)S(1)}, f32[128,512]{1,0:T(8,128)}, u32[]{:S(2)}, u32[]{:S(2)}) %collective-permute-start.9) | collective-permute-done | bytes 262176 | tf_op jit(solution)/shard_map/ppermute | solution.py:10
  195.6 2.0 pad_maximum_fusion.28
  198.7 16.2 %collective-permute-start.10 = (f32[128,512]{1,0:T(8,128)S(1)}, f32[128,512]{1,0:T(8,128)S(1)}, u32[]{:S(2)}, u32[]{:S(2)}) collective-permute-start(f32[128,512]{1,0:T(8,128)S(1)} %get-tuple-element.76), channel_id=1, source_target_pairs={{0,1},{1,2},{2,3},{3,4},{4,5},{5,6},{6,7},{7,8},{8,9},{9,10},{10,1... | collective-permute-start | bytes 786440 | tf_op jit(solution)/shard_map/ppermute | solution.py:10
  214.8 1.9 collective-permute-start.11
  216.8 10.4 %collective-permute-done.10 = f32[128,512]{1,0:T(8,128)S(1)} collective-permute-done((f32[128,512]{1,0:T(8,128)S(1)}, f32[128,512]{1,0:T(8,128)S(1)}, u32[]{:S(2)}, u32[]{:S(2)}) %collective-permute-start.10) | collective-permute-done | bytes 262176 | tf_op jit(solution)/shard_map/ppermute | solution.py:10
  227.2 11.8 %collective-permute-done.11 = f32[128,512]{1,0:T(8,128)S(1)} collective-permute-done((f32[128,512]{1,0:T(8,128)S(1)}, f32[128,512]{1,0:T(8,128)S(1)}, u32[]{:S(2)}, u32[]{:S(2)}) %collective-permute-start.11) | collective-permute-done | bytes 262176 | tf_op jit(solution)/shard_map/ppermute | solution.py:10
  (35 shorter events, 21.2 us)
Async XLA Ops:
  6.5 48.7 %all-gather.2.cloned.1.call-start = ((), (), s32[]{:S(2)}) async-start(), calls=%async_computation | async-start | bytes 4456448 | tf_op jit(solution)/shard_map/all_gather | solution.py:37
  7.3 17.0 %collective-permute-start = (f32[128,512]{1,0:T(8,128)}, f32[128,512]{1,0:T(8,128)S(1)}, u32[]{:S(2)}, u32[]{:S(2)}) collective-permute-start(f32[128,512]{1,0:T(8,128)} %param.9), channel_id=1, source_target_pairs={{1,0},{2,1},{3,2},{4,3},{5,4},{6,5},{7,6},{8,7},{9,8},{10,9},{11,1... | collective-permute-start | bytes 786440 | tf_op jit(solution)/shard_map/ppermute | solution.py:10
  9.2 24.0 %collective-permute-start.1 = (f32[128,512]{1,0:T(8,128)}, f32[128,512]{1,0:T(8,128)S(1)}, u32[]{:S(2)}, u32[]{:S(2)}) collective-permute-start(f32[128,512]{1,0:T(8,128)} %param.9), channel_id=1, source_target_pairs={{2,0},{3,1},{4,2},{5,3},{6,4},{7,5},{8,6},{9,7},{10,8},{11,9},{12,... | collective-permute-start | bytes 786440 | tf_op jit(solution)/shard_map/ppermute | solution.py:10
  33.2 0.9 copy-start.2
  60.8 29.9 %collective-permute-start.2 = (f32[128,512]{1,0:T(8,128)}, f32[128,512]{1,0:T(8,128)S(1)}, u32[]{:S(2)}, u32[]{:S(2)}) collective-permute-start(f32[128,512]{1,0:T(8,128)} %get-tuple-element.80), channel_id=1, source_target_pairs={{0,1},{1,2},{2,3},{3,4},{4,5},{5,6},{6,7},{7,8},{8,9},{9,10},{10,1... | collective-permute-start | bytes 786440 | tf_op jit(solution)/shard_map/ppermute | solution.py:10
  64.3 46.8 %collective-permute-start.3 = (f32[128,512]{1,0:T(8,128)}, f32[128,512]{1,0:T(8,128)}, u32[]{:S(2)}, u32[]{:S(2)}) collective-permute-start(f32[128,512]{1,0:T(8,128)} %get-tuple-element.79), channel_id=1, source_target_pairs={{0,2},{1,3},{2,4},{3,5},{4,6},{5,7},{6,8},{7,9},{8,10},{9,11},{10,... | collective-permute-start | bytes 786440 | tf_op jit(solution)/shard_map/ppermute | solution.py:10
  90.6 0.7 copy-start.8
  112.3 20.9 %copy-start.6 = (f32[128,512]{1,0:T(8,128)}, f32[128,512]{1,0:T(8,128)S(1)}, u32[]{:S(2)}) copy-start(f32[128,512]{1,0:T(8,128)S(1)} %fusion.38) | copy-start | bytes 786436
  112.3 13.6 %collective-permute-start.4 = (f32[128,512]{1,0:T(8,128)S(1)}, f32[128,512]{1,0:T(8,128)}, u32[]{:S(2)}, u32[]{:S(2)}) collective-permute-start(f32[128,512]{1,0:T(8,128)S(1)} %fusion.38), channel_id=1, source_target_pairs={{1,0},{2,1},{3,2},{4,3},{5,4},{6,5},{7,6},{8,7},{9,8},{10,9},{11,1... | collective-permute-start | bytes 786440 | tf_op jit(solution)/shard_map/ppermute | solution.py:10
  114.2 16.9 %collective-permute-start.5 = (f32[128,512]{1,0:T(8,128)S(1)}, f32[128,512]{1,0:T(8,128)}, u32[]{:S(2)}, u32[]{:S(2)}) collective-permute-start(f32[128,512]{1,0:T(8,128)S(1)} %fusion.38), channel_id=1, source_target_pairs={{2,0},{3,1},{4,2},{5,3},{6,4},{7,5},{8,6},{9,7},{10,8},{11,9},{12,... | collective-permute-start | bytes 786440 | tf_op jit(solution)/shard_map/ppermute | solution.py:10
  135.5 5.8 %slice-start.1 = ((f32[128,512]{1,0:T(8,128)}), f32[128,256]{1,0:T(8,128)S(1)}, s32[]{:S(2)}) async-start(f32[128,512]{1,0:T(8,128)} %fusion.18), calls=%async_computation.2 | async-start | bytes 262144 | tf_op jit(solution)/shard_map/cond/branch_1_fun/slice | solution.py:21
  140.6 0.7 copy-start.4
  153.0 13.1 %collective-permute-start.6 = (f32[128,512]{1,0:T(8,128)}, f32[128,512]{1,0:T(8,128)S(1)}, u32[]{:S(2)}, u32[]{:S(2)}) collective-permute-start(f32[128,512]{1,0:T(8,128)} %get-tuple-element.78), channel_id=1, source_target_pairs={{0,1},{1,2},{2,3},{3,4},{4,5},{5,6},{6,7},{7,8},{8,9},{9,10},{10,1... | collective-permute-start | bytes 786440 | tf_op jit(solution)/shard_map/ppermute | solution.py:10
  154.9 21.3 %collective-permute-start.7 = (f32[128,512]{1,0:T(8,128)}, f32[128,512]{1,0:T(8,128)}, u32[]{:S(2)}, u32[]{:S(2)}) collective-permute-start(f32[128,512]{1,0:T(8,128)} %get-tuple-element.77), channel_id=1, source_target_pairs={{0,2},{1,3},{2,4},{3,5},{4,6},{5,7},{6,8},{7,9},{8,10},{9,11},{10,... | collective-permute-start | bytes 786440 | tf_op jit(solution)/shard_map/ppermute | solution.py:10
  166.1 0.7 copy-start.7
  177.3 20.2 %copy-start.5 = (f32[128,512]{1,0:T(8,128)}, f32[128,512]{1,0:T(8,128)S(1)}, u32[]{:S(2)}) copy-start(f32[128,512]{1,0:T(8,128)S(1)} %fusion.37) | copy-start | bytes 786436
  177.3 14.4 %collective-permute-start.8 = (f32[128,512]{1,0:T(8,128)S(1)}, f32[128,512]{1,0:T(8,128)}, u32[]{:S(2)}, u32[]{:S(2)}) collective-permute-start(f32[128,512]{1,0:T(8,128)S(1)} %fusion.37), channel_id=1, source_target_pairs={{1,0},{2,1},{3,2},{4,3},{5,4},{6,5},{7,6},{8,7},{9,8},{10,9},{11,1... | collective-permute-start | bytes 786440 | tf_op jit(solution)/shard_map/ppermute | solution.py:10
  179.5 16.1 %collective-permute-start.9 = (f32[128,512]{1,0:T(8,128)S(1)}, f32[128,512]{1,0:T(8,128)}, u32[]{:S(2)}, u32[]{:S(2)}) collective-permute-start(f32[128,512]{1,0:T(8,128)S(1)} %fusion.37), channel_id=1, source_target_pairs={{2,0},{3,1},{4,2},{5,3},{6,4},{7,5},{8,6},{9,7},{10,8},{11,9},{12,... | collective-permute-start | bytes 786440 | tf_op jit(solution)/shard_map/ppermute | solution.py:10
  198.7 28.6 %collective-permute-start.10 = (f32[128,512]{1,0:T(8,128)S(1)}, f32[128,512]{1,0:T(8,128)S(1)}, u32[]{:S(2)}, u32[]{:S(2)}) collective-permute-start(f32[128,512]{1,0:T(8,128)S(1)} %get-tuple-element.76), channel_id=1, source_target_pairs={{0,1},{1,2},{2,3},{3,4},{4,5},{5,6},{6,7},{7,8},{8,9},{9,10},{10,1... | collective-permute-start | bytes 786440 | tf_op jit(solution)/shard_map/ppermute | solution.py:10
  214.8 24.2 %collective-permute-start.11 = (f32[128,512]{1,0:T(8,128)S(1)}, f32[128,512]{1,0:T(8,128)S(1)}, u32[]{:S(2)}, u32[]{:S(2)}) collective-permute-start(f32[128,512]{1,0:T(8,128)S(1)} %get-tuple-element.75), channel_id=1, source_target_pairs={{0,2},{1,3},{2,4},{3,5},{4,6},{5,7},{6,8},{7,9},{8,10},{9,11},{10,... | collective-permute-start | bytes 786440 | tf_op jit(solution)/shard_map/ppermute | solution.py:10
Sparse Core Ops, SparseCore 0:
  9.5 45.7 all-gather.1
where the time goes:
time: 249 us; the launch traced here: 248 us
  waiting for transfers between devices  119 us (48%)
  starting transfers between devices  75.3 us (30%)
  local copies, waits for them, and re-layouts  17.8 us (7%)
  other arithmetic  14.3 us (6%)
  between operations  14.3 us (6%)
  matrix products  6.76 us (3%)
    ppermute x12, waiting for transfers between devices, passed_along(): return lax.ppermute(block, axis, route)  97.3 us
    ppermute x12, starting transfers between devices, passed_along(): return lax.ppermute(block, axis, route)  75.3 us
    all_gather x1, waiting for transfers between devices, on_device(): gathered = lax.all_gather(factors, 'row', axis=2, tiled=True)  21.1 us
    dot_general x4, matrix products, product(): jnp.dot(former, latter, precision=lax.Precision.HIGHEST, preferred_elemen...  6.76 us
  transfers between devices with their start and end apart: 13, of which 12 were waited for; matrix products, arithmetic and copies ran while one was open for 1% of the time, Pallas kernels for 0%

commit v1 on v0

v1 whole, which is shorter than its diff:
```python
import functools

import jax
import jax.numpy as jnp
from jax import lax
from jax.experimental import pallas as pl
from jax.experimental.pallas import tpu as pltpu
from jax.sharding import PartitionSpec as P

MESH = pl.DeviceIdType.MESH


def kernel(groups, vec, fac, off, out, fetched, gather, hop, whi, wlo, own, one, two, right1, right2, left, last,
           gsend, grecv, ssend, srecv, zsend, zrecv, vsend, vrecv, fsem):
    row = lax.axis_index("row")
    col = lax.axis_index("col")
    half = own.shape[2]
    core = lax.rem(row, 2)
    chip = row // 2
    x = lax.rem(chip, 4)
    y = chip // 4
    place = lax.rem(col, 3)
    has_left = col > 0
    has_right = col < groups - 1
    xnext = y * 4 + lax.rem(x + 1, 4)
    xprev = y * 4 + lax.rem(x + 3, 4)
    xfar = y * 4 + lax.rem(x + 2, 4)
    other = (1 - y) * 4
    ychip = other + x
    sibling = chip * 2 + (1 - core)

    fetches = [
        pltpu.make_async_copy(fac, fetched, fsem.at[0]),
        pltpu.make_async_copy(vec.at[:, pl.ds(0, half)], own.at[0], fsem.at[1]),
        pltpu.make_async_copy(vec.at[:, pl.ds(half, half)], own.at[1], fsem.at[2]),
    ]
    for fetch in fetches:
        fetch.start()

    barrier = pltpu.get_barrier_semaphore()

    def greet(r, c):
        pl.semaphore_signal(barrier, inc=1, device_id=(r, c), device_id_type=MESH)

    for c in (xnext, xprev, ychip):
        greet(c * 2 + core, col)
    greet(sibling, col)

    @pl.when(has_left)
    def _():
        greet(row, col - 1)

    @pl.when(has_right)
    def _():
        greet(row, col + 1)

    for fetch in fetches:
        fetch.wait()
    shift = off[col] > 0
    f0, f1, f2, f3 = fetched[0, 0], fetched[0, 1], fetched[0, 2], fetched[0, 3]
    gather[0, chip, core] = f0
    gather[1, chip, core] = jnp.where(shift, f0, f1)
    hop[0] = jnp.where(shift, f1, f2)
    hop[1] = jnp.where(shift, f2, f3)
    hop[2] = f3

    pl.semaphore_wait(barrier, 4 + has_left.astype(jnp.int32) + has_right.astype(jnp.int32))

    def hop_copy(i):
        return pltpu.make_async_remote_copy(
            hop.at[i], gather.at[i + 2, chip, core], zsend.at[i], zrecv.at[i],
            device_id=(row, col + 1), device_id_type=MESH)

    @pl.when(has_right)
    def _():
        for i in range(3):
            hop_copy(i).start()

    def vcopy(src, dst, slot, landing, to):
        return pltpu.make_async_remote_copy(
            src, dst, vsend.at[slot], vrecv.at[landing], device_id=(row, to), device_id_type=MESH)

    def loan_half():
        return vcopy(own.at[0], right1.at[0], 0, 0, col - 1)

    def loan_block():
        return vcopy(own, right1, 0, 0, col - 1)

    @pl.when(place == 1)
    def _():
        loan_half().start()

    @pl.when(place == 2)
    def _():
        loan_block().start()

    def shard(f, s, to, slot):
        return pltpu.make_async_remote_copy(
            gather.at[f, s, core], gather.at[f, s, core], gsend.at[f, slot], grecv.at[f, s],
            device_id=(to * 2 + core, col), device_id_type=MESH)

    def got(f, s):
        shard(f, s, xnext, 0).wait_recv()

    def step_one(f):
        @pl.when(f >= 2)
        def _():
            hop_copy(f - 2).wait_recv()

        shard(f, chip, ychip, 0).start()
        shard(f, chip, xnext, 1).start()
        shard(f, chip, xprev, 2).start()

    def step_two(f):
        @pl.when(core == 0)
        def _():
            up = lax.rem(f, 2) == 0
            got(f, xprev)
            shard(f, xprev, ychip, 3).start()

            @pl.when(up)
            def _():
                shard(f, xprev, xnext, 4).start()

            got(f, xnext)
            shard(f, xnext, ychip, 5).start()

            @pl.when(jnp.logical_not(up))
            def _():
                shard(f, xnext, xprev, 4).start()

        @pl.when(core == 1)
        def _():
            got(f, ychip)
            shard(f, ychip, xnext, 3).start()
            shard(f, ychip, xprev, 4).start()
            got(f, xprev)
            shard(f, xprev, xnext, 5).start()

    def step_three(f):
        @pl.when(core == 0)
        def _():
            got(f, xfar)
            shard(f, xfar, ychip, 6).start()

        @pl.when(core == 1)
        def _():
            relayed = other + lax.rem(x + 1, 4)
            got(f, relayed)
            shard(f, relayed, xprev, 6).start()

    def to_sibling(f):
        return pltpu.make_async_remote_copy(
            gather.at[f, :, core], gather.at[f, :, core], ssend.at[f], srecv.at[f],
            device_id=(sibling, col), device_id_type=MESH)

    def from_sibling(f):
        return pltpu.make_async_remote_copy(
            gather.at[f, :, 1 - core], gather.at[f, :, 1 - core], ssend.at[f], srecv.at[f],
            device_id=(sibling, col), device_id_type=MESH)

    def step_four(f):
        @pl.when(core == 0)
        def _():
            for i in range(4):
                got(f, other + i)

        @pl.when(core == 1)
        def _():
            got(f, xnext)
            got(f, xfar)
            got(f, other + lax.rem(x + 2, 4))
            got(f, other + lax.rem(x + 3, 4))

        to_sibling(f).start()

    def step_five(f):
        from_sibling(f).wait_recv()

        def split(i, carry):
            for k in range(2):
                g = gather[f, i, k]
                hi = g.astype(jnp.bfloat16)
                whi[f, 2 * i + k] = hi
                wlo[f, 2 * i + k] = (g - hi.astype(jnp.float32)).astype(jnp.bfloat16)
            return carry

        lax.fori_loop(0, 8, split, 0)

    def each(step, lo, hi):
        def body(f, carry):
            step(f)
            return carry

        lax.fori_loop(lo, hi, body, 0)

    wide = 2 * half
    hr = has_right.astype(jnp.int32)
    keep_first = 1 - off[col]
    keep_fifth = hr * off[jnp.maximum(col - 1, 0)]

    def products(work, lo, hi):
        def body(j, carry):
            pos = j - jnp.where(j >= 2, 2, 0)
            use = jnp.where(j == 0, keep_first, jnp.where(j == 2, 1, jnp.where(j == 4, keep_fifth, hr)))
            halves = [work[pos], work[pos + 1]]
            full = jnp.concatenate(halves, 1)
            hi_part = full.astype(jnp.bfloat16)
            lo_part = (full - hi_part.astype(jnp.float32)).astype(jnp.bfloat16)
            both = jnp.concatenate([hi_part, lo_part], 0)
            rows = full.shape[0]
            for n in range(2):
                wh = whi[j, :, :, n * half:(n + 1) * half].reshape(wide, half)
                wl = wlo[j, :, :, n * half:(n + 1) * half].reshape(wide, half)
                big = jnp.dot(both, wh, preferred_element_type=jnp.float32)
                small = jnp.dot(hi_part, wl, preferred_element_type=jnp.float32)
                result = big[:rows] + (big[rows:] + small)
                work[pos + n] = jnp.where(use > 0, result, halves[n])
            return carry

        lax.fori_loop(lo, hi, body, 0)

    has_b = has_left
    first = place == 0
    total = jnp.where(has_b, 5, 2)
    split_at = jnp.where(first, 2, 5)
    for step in (step_one, step_two, step_three):
        each(step, 0, split_at)
    later = jnp.maximum(total, split_at)
    each(step_one, split_at, later)
    each(step_four, 0, split_at)
    each(step_five, 0, split_at)

    @pl.when(jnp.logical_not(has_right))
    def _():
        right1[...] = jnp.zeros(right1.shape, jnp.float32)

    def arrived(dst, landing):
        vcopy(dst, dst, 0, landing, col).wait_recv()

    @pl.when(first)
    def _():
        one[0] = own[0]
        one[1] = own[1]

        arrived(right1.at[0], 0)
        one[2] = right1[0]

    @pl.when(place == 1)
    def _():
        @pl.when(has_right)
        def _():
            arrived(right1, 0)

        one[1] = own[1]
        one[2] = right1[0]
        one[3] = right1[1]
        arrived(left.at[0], 2)
        one[0] = left[0]

    @pl.when(place == 2)
    def _():
        arrived(right1, 0)
        one[2] = right1[0]
        one[3] = right1[1]
        arrived(left.at[1], 3)
        one[1] = left[1]
        arrived(left.at[0], 2)
        one[0] = left[0]

    products(one, jnp.where(first, 0, 2), jnp.where(first, 2, 5))

    def first_half_right(work):
        return vcopy(work.at[2], left.at[0], 1, 2, col + 1)

    def second_half_right():
        return vcopy(one.at[3], left.at[1], 2, 3, col + 1)

    def early_left():
        return vcopy(one.at[pl.ds(0, 2)], right1, 3, 0, col - 1)

    def late_left():
        return vcopy(two.at[pl.ds(0, 2)], right2, 3, 1, col - 1)

    def last_right():
        return vcopy(two.at[pl.ds(2, 2)], last, 4, 4, col + 1)

    @pl.when(first)
    def _():
        @pl.when(has_right)
        def _():
            first_half_right(one).start()

        @pl.when(has_left)
        def _():
            early_left().start()

    @pl.when(jnp.logical_and(place > 0, has_right))
    def _():
        second_half_right().start()

    for step in (step_two, step_three, step_four, step_five):
        each(step, split_at, later)

    @pl.when(jnp.logical_and(first, has_b))
    def _():
        @pl.when(has_right)
        def _():
            arrived(right2, 1)

        two[2] = right2[0]
        two[3] = right2[1]
        arrived(left.at[1], 3)
        two[1] = left[1]
        arrived(left.at[0], 2)
        two[0] = left[0]

    @pl.when(place > 0)
    def _():
        two[0] = one[0]
        two[1] = one[1]
        two[2] = one[2]

    products(two, jnp.where(first, 2, 0), jnp.where(first, total, 2))

    def give(ref):
        out[:, :half] = ref[0]
        out[:, half:] = ref[1]

    @pl.when(jnp.logical_and(first, has_b))
    def _():
        @pl.when(has_right)
        def _():
            last_right().start()

        give(two)

    @pl.when(col == 0)
    def _():
        give(one)

    @pl.when(place > 0)
    def _():
        @pl.when(has_right)
        def _():
            first_half_right(two).start()

    @pl.when(jnp.logical_and(place == 1, col > 1))
    def _():
        late_left().start()
        arrived(last, 4)
        give(last)

    @pl.when(jnp.logical_or(place == 2, col == 1))
    def _():
        give(two)

    @pl.when(has_right)
    def _():
        for i in range(3):
            hop_copy(i).wait_send()
        first_half_right(two).wait_send()

    @pl.when(place == 1)
    def _():
        loan_half().wait_send()

    @pl.when(place == 2)
    def _():
        loan_block().wait_send()

    @pl.when(jnp.logical_and(place > 0, has_right))
    def _():
        second_half_right().wait_send()

    @pl.when(jnp.logical_and(first, has_left))
    def _():
        early_left().wait_send()

        @pl.when(has_right)
        def _():
            last_right().wait_send()

    @pl.when(jnp.logical_and(place == 1, col > 1))
    def _():
        late_left().wait_send()

    def drain(f, carry):
        for slot in range(7):
            shard(f, chip, xnext, slot).wait_send()
        to_sibling(f).wait_send()
        return carry

    lax.fori_loop(0, total, drain, 0)


def on_device(vectors, factors, offsets):
    rows, cols = vectors.shape
    half = cols // 2
    depth = factors.shape[2]
    f32, dma = jnp.float32, pltpu.SemaphoreType.DMA
    in_vmem = pl.BlockSpec(memory_space=pltpu.VMEM)
    in_place = pl.BlockSpec(memory_space=pltpu.HBM)
    return pl.pallas_call(
        functools.partial(kernel, lax.axis_size("col")),
        out_shape=jax.ShapeDtypeStruct((rows, cols), f32),
        in_specs=[in_place, in_place, pl.BlockSpec(memory_space=pltpu.SMEM)],
        out_specs=in_vmem,
        scratch_shapes=[
            pltpu.VMEM((1, 4, depth, cols), f32),
            pltpu.VMEM((5, 8, 2, depth, cols), f32),
            pltpu.VMEM((3, depth, cols), f32),
            pltpu.VMEM((5, 16, depth, cols), jnp.bfloat16),
            pltpu.VMEM((5, 16, depth, cols), jnp.bfloat16),
            pltpu.VMEM((2, rows, half), f32),
            pltpu.VMEM((4, rows, half), f32),
            pltpu.VMEM((4, rows, half), f32),
            pltpu.VMEM((2, rows, half), f32),
            pltpu.VMEM((2, rows, half), f32),
            pltpu.VMEM((2, rows, half), f32),
            pltpu.VMEM((2, rows, half), f32),
            dma((5, 7)), dma((5, 8)), dma((5,)), dma((5,)), dma((3,)), dma((3,)), dma((5,)), dma((5,)), dma((3,)),
        ],
        compiler_params=pltpu.CompilerParams(
            collective_id=0, has_side_effects=True, vmem_limit_bytes=60 << 20),
    )(vectors, factors, offsets)


def solution(mesh):
    placed = (P("row", "col"), P("col", None, "row", None), P())
    return jax.shard_map(
        on_device, mesh=mesh, in_specs=placed, out_specs=P("row", "col"), check_vma=False
    )
```

time: 249 us -> 71 us (0.29)
  the two profiles are of different devices: /device:TPU:112 before, /device:TPU:32 now
where the time goes in v1:
time: 71 us; the launch traced here: 70.8 us
  Pallas kernels  69.2 us (97%)
  local copies, waits for them, and re-layouts  1.67 us (2%)
    pallas_call x1, Pallas kernels, on_device(): pl.pallas_call(functools.partial(kernel, lax.axis_size('col')), out_shape...  69.2 us
    unnamed x1, local copies, waits for them, and re-layouts  1.67 us

profile of v1, /device:TPU:32, one launch (start us, length us, event | category | flops | bytes accessed | tf_op | source)
XLA Modules:
  0.0 70.8 jit_solution(11747335045810609820)
XLA Ops:
  0.0 69.2 %shard_map.37 = f32[128,512]{1,0:T(8,128)} custom-call(f32[128,512]{1,0:T(8,128)} %vec.1, f32[1,4,32,512]{3,2,1,0:T(8,128)} %fac.1, s32[32]{0:T(128)} %off.1), custom_call_target="tpu_custom_call" | custom-call | tf_op jit(solution)/shard_map/pallas_call | solution.py:404
  69.2 1.7 %copy.5 = f32[128,512]{1,0:T(8,128)} copy(f32[128,512]{1,0:T(8,128)} %shard_map.37) | data formatting | bytes 524288

commit v2 on v1

v2 whole, which is shorter than its diff:
```python
import functools

import jax
import jax.numpy as jnp
from jax import lax
from jax.experimental import pallas as pl
from jax.experimental.pallas import tpu as pltpu
from jax.sharding import PartitionSpec as P

MESH = pl.DeviceIdType.MESH
PARTS = 4


def kernel(groups, vec, fac, off, out, fetched, gather, hop, whi, wlo, own, one, two, right1, right2, left, last,
           gsend, grecv, ssend, srecv, zsend, zrecv, vsend, vrecv, fsem):
    row = lax.axis_index("row")
    col = lax.axis_index("col")
    half = own.shape[2]
    core = lax.rem(row, 2)
    chip = row // 2
    x = lax.rem(chip, 4)
    y = chip // 4
    place = lax.rem(col, 3)
    has_left = col > 0
    has_right = col < groups - 1
    xnext = y * 4 + lax.rem(x + 1, 4)
    xprev = y * 4 + lax.rem(x + 3, 4)
    xfar = y * 4 + lax.rem(x + 2, 4)
    other = (1 - y) * 4
    ychip = other + x
    sibling = chip * 2 + (1 - core)

    fetches = [
        pltpu.make_async_copy(fac, fetched, fsem.at[0]),
        pltpu.make_async_copy(vec.at[:, pl.ds(0, half)], own.at[0], fsem.at[1]),
        pltpu.make_async_copy(vec.at[:, pl.ds(half, half)], own.at[1], fsem.at[2]),
    ]
    for fetch in fetches:
        fetch.start()

    barrier = pltpu.get_barrier_semaphore()

    def greet(r, c):
        pl.semaphore_signal(barrier, inc=1, device_id=(r, c), device_id_type=MESH)

    for c in (xnext, xprev, ychip):
        greet(c * 2 + core, col)
    greet(sibling, col)

    @pl.when(has_left)
    def _():
        greet(row, col - 1)

    @pl.when(has_right)
    def _():
        greet(row, col + 1)

    for fetch in fetches:
        fetch.wait()
    for i in range(2):
        gather[i, chip, core] = fetched[0, i]
        hop[i] = fetched[0, i + 2]

    pl.semaphore_wait(barrier, 4 + has_left.astype(jnp.int32) + has_right.astype(jnp.int32))

    def hop_copy(i):
        return pltpu.make_async_remote_copy(
            hop.at[i], gather.at[i + 2, chip, core], zsend.at[i], zrecv.at[i],
            device_id=(row, col + 1), device_id_type=MESH)

    @pl.when(has_right)
    def _():
        for i in range(2):
            hop_copy(i).start()

    def vcopy(src, dst, slot, landing, to, part=0):
        return pltpu.make_async_remote_copy(
            src, dst, vsend.at[slot, part], vrecv.at[landing, part], device_id=(row, to), device_id_type=MESH)

    def loan_block():
        return vcopy(own, right1, 0, 0, col - 1)

    @pl.when(place > 0)
    def _():
        loan_block().start()

    def shard(f, s, to, slot):
        return pltpu.make_async_remote_copy(
            gather.at[f, s, core], gather.at[f, s, core], gsend.at[f, slot], grecv.at[f, s],
            device_id=(to * 2 + core, col), device_id_type=MESH)

    def got(f, s):
        shard(f, s, xnext, 0).wait_recv()

    def step_one(f):
        @pl.when(f >= 2)
        def _():
            hop_copy(f - 2).wait_recv()

        shard(f, chip, ychip, 0).start()
        shard(f, chip, xnext, 1).start()
        shard(f, chip, xprev, 2).start()

    def step_two(f):
        @pl.when(core == 0)
        def _():
            up = lax.rem(f, 2) == 0
            got(f, xprev)
            shard(f, xprev, ychip, 3).start()

            @pl.when(up)
            def _():
                shard(f, xprev, xnext, 4).start()

            got(f, xnext)
            shard(f, xnext, ychip, 5).start()

            @pl.when(jnp.logical_not(up))
            def _():
                shard(f, xnext, xprev, 4).start()

        @pl.when(core == 1)
        def _():
            got(f, ychip)
            shard(f, ychip, xnext, 3).start()
            shard(f, ychip, xprev, 4).start()
            got(f, xprev)
            shard(f, xprev, xnext, 5).start()

    def step_three(f):
        @pl.when(core == 0)
        def _():
            got(f, xfar)
            shard(f, xfar, ychip, 6).start()

        @pl.when(core == 1)
        def _():
            relayed = other + lax.rem(x + 1, 4)
            got(f, relayed)
            shard(f, relayed, xprev, 6).start()

    def to_sibling(f):
        return pltpu.make_async_remote_copy(
            gather.at[f, :, core], gather.at[f, :, core], ssend.at[f], srecv.at[f],
            device_id=(sibling, col), device_id_type=MESH)

    def from_sibling(f):
        return pltpu.make_async_remote_copy(
            gather.at[f, :, 1 - core], gather.at[f, :, 1 - core], ssend.at[f], srecv.at[f],
            device_id=(sibling, col), device_id_type=MESH)

    def step_four(f):
        @pl.when(core == 0)
        def _():
            for i in range(4):
                got(f, other + i)

        @pl.when(core == 1)
        def _():
            got(f, xnext)
            got(f, xfar)
            got(f, other + lax.rem(x + 2, 4))
            got(f, other + lax.rem(x + 3, 4))

        to_sibling(f).start()

    def step_five(f):
        from_sibling(f).wait_recv()

        def split(i, carry):
            for k in range(2):
                g = gather[f, i, k]
                hi = g.astype(jnp.bfloat16)
                whi[f, 2 * i + k] = hi
                wlo[f, 2 * i + k] = (g - hi.astype(jnp.float32)).astype(jnp.bfloat16)
            return carry

        lax.fori_loop(0, 8, split, 0)

    def each(step, lo, hi):
        def body(f, carry):
            step(f)
            return carry

        lax.fori_loop(lo, hi, body, 0)

    wide = 2 * half
    hr = has_right.astype(jnp.int32)

    def products(work, lo, hi, rows):
        def body(j, carry):
            k = lax.rem(j, 2)
            moved = off[jnp.where(j < 2, col, jnp.maximum(col - 1, 0))]
            use = jnp.where(k == 0, jnp.maximum(hr, 1 - moved), hr) > 0
            moved = moved > 0
            first, second, third = (work[k + n, rows, :] for n in range(3))
            halves = [jnp.where(moved, second, first), jnp.where(moved, third, second)]
            full = jnp.concatenate(halves, 1)
            hi_part = full.astype(jnp.bfloat16)
            lo_part = (full - hi_part.astype(jnp.float32)).astype(jnp.bfloat16)
            both = jnp.concatenate([hi_part, lo_part], 0)
            count = full.shape[0]
            results = []
            for n in range(2):
                wh = whi[j, :, :, n * half:(n + 1) * half].reshape(wide, half)
                wl = wlo[j, :, :, n * half:(n + 1) * half].reshape(wide, half)
                big = jnp.dot(both, wh, preferred_element_type=jnp.float32)
                small = jnp.dot(hi_part, wl, preferred_element_type=jnp.float32)
                results.append(jnp.where(use, big[:count] + (big[count:] + small), halves[n]))
            work[k, rows, :] = jnp.where(moved, first, results[0])
            work[k + 1, rows, :] = jnp.where(moved, results[0], results[1])
            work[k + 2, rows, :] = jnp.where(moved, results[1], third)
            return carry

        lax.fori_loop(lo, hi, body, 0)

    first = place == 0
    total = jnp.where(has_left, 4, 2)

    each(step_one, 0, 2)

    def second_round(f):
        step_two(f)

        @pl.when(place > 0)
        def _():
            step_one(f + 2)

    def third_round(f):
        step_three(f)

        @pl.when(place > 0)
        def _():
            step_two(f + 2)

    def fourth_round(f):
        step_three(f)
        step_four(f - 2)

        @pl.when(f > 2)
        def _():
            step_five(f - 3)

    def fifth_round(f):
        step_four(f)
        step_five(f - 1)

    each(second_round, 0, 2)

    each(third_round, 0, 2)

    @pl.when(place > 0)
    def _():
        each(fourth_round, 2, 4)
        each(fifth_round, 2, 4)
        step_five(3)

    @pl.when(first)
    def _():
        each(step_four, 0, 2)
        each(step_five, 0, 2)

    @pl.when(jnp.logical_not(has_right))
    def _():
        right1[...] = jnp.zeros(right1.shape, jnp.float32)
        right2[...] = jnp.zeros(right2.shape, jnp.float32)

    length = own.shape[1] // PARTS

    def rows_of(part):
        return pl.ds(pl.multiple_of(part * length, length), length)

    def arrived(dst, landing, part=0):
        vcopy(dst, dst, 0, landing, col, part).wait_recv()

    def left_back(part):
        arrived(left.at[:, rows_of(part)], 2, part)

    def block_right(part):
        return vcopy(one.at[pl.ds(2, 2), rows_of(part)], left.at[:, rows_of(part)], 1, 2, col + 1, part)

    def early_left():
        return vcopy(one.at[pl.ds(0, 2)], right1, 2, 0, col - 1)

    def late_left(part):
        return vcopy(one.at[pl.ds(0, 2), rows_of(part)], right2.at[:, rows_of(part)], 2, 1, col - 1, part)

    def last_right(part):
        return vcopy(two.at[pl.ds(2, 2), rows_of(part)], last.at[:, rows_of(part)], 3, 3, col + 1, part)

    lends_late = jnp.logical_and(place == 1, col > 1)

    @pl.when(has_right)
    def _():
        arrived(right1, 0)

    one[0] = own[0]
    one[1] = own[1]
    one[2] = right1[0]
    one[3] = right1[1]

    def first_stage(part):
        rows = rows_of(part)

        @pl.when(place > 0)
        def _():
            left_back(part)

            one[0, rows, :] = left[0, rows, :]
            one[1, rows, :] = left[1, rows, :]

            products(one, 2, 4, rows)

        products(one, 0, 2, rows)

        @pl.when(has_right)
        def _():
            block_right(part).start()

        @pl.when(lends_late)
        def _():
            late_left(part).start()

    each(first_stage, 0, PARTS)

    @pl.when(jnp.logical_and(first, has_left))
    def _():
        early_left().start()

        for step in (step_one, step_two, step_three, step_four, step_five):
            each(step, 2, total)

        def second_stage(part):
            rows = rows_of(part)

            @pl.when(has_right)
            def _():
                arrived(right2.at[:, rows], 1, part)

            left_back(part)
            two[0, rows, :] = left[0, rows, :]
            two[1, rows, :] = left[1, rows, :]
            two[2, rows, :] = right2[0, rows, :]
            two[3, rows, :] = right2[1, rows, :]
            products(two, 2, 4, rows)

            @pl.when(has_right)
            def _():
                last_right(part).start()

        each(second_stage, 0, PARTS)

    def give(ref):
        out[:, :half] = ref[0]
        out[:, half:] = ref[1]

    @pl.when(lends_late)
    def _():
        for part in range(PARTS):
            arrived(last.at[:, rows_of(part)], 3, part)
        give(last)

    @pl.when(jnp.logical_and(first, has_left))
    def _():
        give(two)

    @pl.when(jnp.logical_or(place == 2, col < 2))
    def _():
        give(one)

    @pl.when(has_right)
    def _():
        for i in range(2):
            hop_copy(i).wait_send()

    @pl.when(place > 0)
    def _():
        loan_block().wait_send()

    @pl.when(jnp.logical_and(first, has_left))
    def _():
        early_left().wait_send()

    def sent(part):
        @pl.when(has_right)
        def _():
            block_right(part).wait_send()

        @pl.when(lends_late)
        def _():
            late_left(part).wait_send()

        @pl.when(jnp.logical_and(jnp.logical_and(first, has_left), has_right))
        def _():
            last_right(part).wait_send()

    each(sent, 0, PARTS)

    def drain(f, carry):
        for slot in range(7):
            shard(f, chip, xnext, slot).wait_send()
        to_sibling(f).wait_send()
        return carry

    lax.fori_loop(0, total, drain, 0)


def on_device(vectors, factors, offsets):
    rows, cols = vectors.shape
    half = cols // 2
    depth = factors.shape[2]
    f32, dma = jnp.float32, pltpu.SemaphoreType.DMA
    in_vmem = pl.BlockSpec(memory_space=pltpu.VMEM)
    in_place = pl.BlockSpec(memory_space=pltpu.HBM)
    return pl.pallas_call(
        functools.partial(kernel, lax.axis_size("col")),
        out_shape=jax.ShapeDtypeStruct((rows, cols), f32),
        in_specs=[in_place, in_place, pl.BlockSpec(memory_space=pltpu.SMEM)],
        out_specs=in_vmem,
        scratch_shapes=[
            pltpu.VMEM((1, 4, depth, cols), f32),
            pltpu.VMEM((4, 8, 2, depth, cols), f32),
            pltpu.VMEM((2, depth, cols), f32),
            pltpu.VMEM((4, 16, depth, cols), jnp.bfloat16),
            pltpu.VMEM((4, 16, depth, cols), jnp.bfloat16),
            pltpu.VMEM((2, rows, half), f32),
            pltpu.VMEM((4, rows, half), f32),
            pltpu.VMEM((4, rows, half), f32),
            pltpu.VMEM((2, rows, half), f32),
            pltpu.VMEM((2, rows, half), f32),
            pltpu.VMEM((2, rows, half), f32),
            pltpu.VMEM((2, rows, half), f32),
            dma((4, 7)), dma((4, 8)), dma((4,)), dma((4,)), dma((2,)), dma((2,)),
            dma((4, PARTS)), dma((4, PARTS)), dma((3,)),
        ],
        compiler_params=pltpu.CompilerParams(
            collective_id=0, has_side_effects=True, vmem_limit_bytes=60 << 20),
    )(vectors, factors, offsets)


def solution(mesh):
    placed = (P("row", "col"), P("col", None, "row", None), P())
    return jax.shard_map(
        on_device, mesh=mesh, in_specs=placed, out_specs=P("row", "col"), check_vma=False
    )
```

time: 71 us -> 64.4 us (0.907)
  the two profiles are of different devices: /device:TPU:32 before, /device:TPU:44 now
where the time goes in v2:
time: 64.4 us; the launch traced here: 63.2 us
  Pallas kernels  61.5 us (95%)
  local copies, waits for them, and re-layouts  1.67 us (3%)
    pallas_call x1, Pallas kernels, on_device(): pl.pallas_call(functools.partial(kernel, lax.axis_size('col')), out_shape...  61.5 us
    unnamed x1, local copies, waits for them, and re-layouts  1.67 us

profile of v2, /device:TPU:44, one launch (start us, length us, event | category | flops | bytes accessed | tf_op | source)
XLA Modules:
  0.0 63.2 jit_solution(9399928613343099918)
XLA Ops:
  0.0 61.5 %shard_map.37 = f32[128,512]{1,0:T(8,128)} custom-call(f32[128,512]{1,0:T(8,128)} %vec.1, f32[1,4,32,512]{3,2,1,0:T(8,128)} %fac.1, s32[32]{0:T(128)} %off.1), custom_call_target="tpu_custom_call" | custom-call | tf_op jit(solution)/shard_map/pallas_call | solution.py:415
  61.5 1.7 %copy.5 = f32[128,512]{1,0:T(8,128)} copy(f32[128,512]{1,0:T(8,128)} %shard_map.37) | data formatting | bytes 524288

commit v3 on v2

--- a/solution.py
+++ b/solution.py
@@ -77,20 +77,37 @@
         return pltpu.make_async_remote_copy(
             src, dst, vsend.at[slot, part], vrecv.at[landing, part], device_id=(row, to), device_id_type=MESH)
 
-    def loan_block():
-        return vcopy(own, right1, 0, 0, col - 1)
+    length = own.shape[1] // PARTS
+
+    def rows_of(part):
+        return pl.ds(pl.multiple_of(part * length, length), length)
+
+    def loan_block(part):
+        return vcopy(own.at[:, rows_of(part)], right1.at[:, rows_of(part)], 0, 0, col - 1, part)
 
     @pl.when(place > 0)
     def _():
-        loan_block().start()
+        for part in range(PARTS):
+            loan_block(part).start()
 
     def shard(f, s, to, slot):
         return pltpu.make_async_remote_copy(
             gather.at[f, s, core], gather.at[f, s, core], gsend.at[f, slot], grecv.at[f, s],
             device_id=(to * 2 + core, col), device_id_type=MESH)
 
+    def to_sibling(f, s):
+        return pltpu.make_async_remote_copy(
+            gather.at[f, s, core], gather.at[f, s, core], ssend.at[f, s], srecv.at[f, s],
+            device_id=(sibling, col), device_id_type=MESH)
+
+    def from_sibling(f, s):
+        return pltpu.make_async_remote_copy(
+            gather.at[f, s, 1 - core], gather.at[f, s, 1 - core], ssend.at[f, s], srecv.at[f, s],
+            device_id=(sibling, col), device_id_type=MESH)
+
     def got(f, s):
         shard(f, s, xnext, 0).wait_recv()
+        to_sibling(f, s).start()
 
     def step_one(f):
         @pl.when(f >= 2)
@@ -100,6 +117,7 @@
         shard(f, chip, ychip, 0).start()
         shard(f, chip, xnext, 1).start()
         shard(f, chip, xprev, 2).start()
+        to_sibling(f, chip).start()
 
     def step_two(f):
         @pl.when(core == 0)
@@ -139,16 +157,6 @@
             got(f, relayed)
             shard(f, relayed, xprev, 6).start()
 
-    def to_sibling(f):
-        return pltpu.make_async_remote_copy(
-            gather.at[f, :, core], gather.at[f, :, core], ssend.at[f], srecv.at[f],
-            device_id=(sibling, col), device_id_type=MESH)
-
-    def from_sibling(f):
-        return pltpu.make_async_remote_copy(
-            gather.at[f, :, 1 - core], gather.at[f, :, 1 - core], ssend.at[f], srecv.at[f],
-            device_id=(sibling, col), device_id_type=MESH)
-
     def step_four(f):
         @pl.when(core == 0)
         def _():
@@ -162,12 +170,9 @@
             got(f, other + lax.rem(x + 2, 4))
             got(f, other + lax.rem(x + 3, 4))
 
-        to_sibling(f).start()
-
     def step_five(f):
-        from_sibling(f).wait_recv()
-
         def split(i, carry):
+            from_sibling(f, i).wait_recv()
             for k in range(2):
                 g = gather[f, i, k]
                 hi = g.astype(jnp.bfloat16)
@@ -265,11 +270,6 @@
         right1[...] = jnp.zeros(right1.shape, jnp.float32)
         right2[...] = jnp.zeros(right2.shape, jnp.float32)
 
-    length = own.shape[1] // PARTS
-
-    def rows_of(part):
-        return pl.ds(pl.multiple_of(part * length, length), length)
-
     def arrived(dst, landing, part=0):
         vcopy(dst, dst, 0, landing, col, part).wait_recv()
 
@@ -279,8 +279,8 @@
     def block_right(part):
         return vcopy(one.at[pl.ds(2, 2), rows_of(part)], left.at[:, rows_of(part)], 1, 2, col + 1, part)
 
-    def early_left():
-        return vcopy(one.at[pl.ds(0, 2)], right1, 2, 0, col - 1)
+    def early_left(part):
+        return vcopy(one.at[pl.ds(0, 2), rows_of(part)], right1.at[:, rows_of(part)], 2, 0, col - 1, part)
 
     def late_left(part):
         return vcopy(one.at[pl.ds(0, 2), rows_of(part)], right2.at[:, rows_of(part)], 2, 1, col - 1, part)
@@ -290,18 +290,19 @@
 
     lends_late = jnp.logical_and(place == 1, col > 1)
 
-    @pl.when(has_right)
-    def _():
-        arrived(right1, 0)
-
     one[0] = own[0]
     one[1] = own[1]
-    one[2] = right1[0]
-    one[3] = right1[1]
 
     def first_stage(part):
         rows = rows_of(part)
 
+        @pl.when(has_right)
+        def _():
+            arrived(right1.at[:, rows], 0, part)
+
+        one[2, rows, :] = right1[0, rows, :]
+        one[3, rows, :] = right1[1, rows, :]
+
         @pl.when(place > 0)
         def _():
             left_back(part)
@@ -325,7 +326,8 @@
 
     @pl.when(jnp.logical_and(first, has_left))
     def _():
-        early_left().start()
+        for part in range(PARTS):
+            early_left(part).start()
 
         for step in (step_one, step_two, step_three, step_four, step_five):
             each(step, 2, total)
@@ -373,15 +375,15 @@
         for i in range(2):
             hop_copy(i).wait_send()
 
-    @pl.when(place > 0)
-    def _():
-        loan_block().wait_send()
-
-    @pl.when(jnp.logical_and(first, has_left))
-    def _():
-        early_left().wait_send()
-
     def sent(part):
+        @pl.when(place > 0)
+        def _():
+            loan_block(part).wait_send()
+
+        @pl.when(jnp.logical_and(first, has_left))
+        def _():
+            early_left(part).wait_send()
+
         @pl.when(has_right)
         def _():
             block_right(part).wait_send()
@@ -399,7 +401,8 @@
     def drain(f, carry):
         for slot in range(7):
             shard(f, chip, xnext, slot).wait_send()
-        to_sibling(f).wait_send()
+        for s in range(8):
+            to_sibling(f, s).wait_send()
         return carry
 
     lax.fori_loop(0, total, drain, 0)
@@ -430,7 +433,7 @@
             pltpu.VMEM((2, rows, half), f32),
             pltpu.VMEM((2, rows, half), f32),
             pltpu.VMEM((2, rows, half), f32),
-            dma((4, 7)), dma((4, 8)), dma((4,)), dma((4,)), dma((2,)), dma((2,)),
+            dma((4, 7)), dma((4, 8)), dma((4, 8)), dma((4, 8)), dma((2,)), dma((2,)),
             dma((4, PARTS)), dma((4, PARTS)), dma((3,)),
         ],
         compiler_params=pltpu.CompilerParams(

time: 64.4 us -> 63.1 us (0.980)
  Pallas kernels: 61.5 us -> 60.8 us
    pallas_call x1, Pallas kernels: 61.5 us -> 60.8 us  [on_device(): pl.pallas_call(functools.partial(kernel, lax.axis_size('col')), out_shape...]
where the time goes in v3:
time: 63.1 us; the launch traced here: 62.5 us
  Pallas kernels  60.8 us (96%)
  local copies, waits for them, and re-layouts  1.67 us (3%)
    pallas_call x1, Pallas kernels, on_device(): pl.pallas_call(functools.partial(kernel, lax.axis_size('col')), out_shape...  60.8 us
    unnamed x1, local copies, waits for them, and re-layouts  1.67 us

profile of v3, /device:TPU:44, one launch (start us, length us, event | category | flops | bytes accessed | tf_op | source)
XLA Modules:
  0.0 62.5 jit_solution(12127813165650490640)
XLA Ops:
  0.0 60.8 %shard_map.37 = f32[128,512]{1,0:T(8,128)} custom-call(f32[128,512]{1,0:T(8,128)} %vec.1, f32[1,4,32,512]{3,2,1,0:T(8,128)} %fac.1, s32[32]{0:T(128)} %off.1), custom_call_target="tpu_custom_call" | custom-call | tf_op jit(solution)/shard_map/pallas_call | solution.py:418
  60.8 1.7 %copy.5 = f32[128,512]{1,0:T(8,128)} copy(f32[128,512]{1,0:T(8,128)} %shard_map.37) | data formatting | bytes 524288

commit v4 on v3

--- a/solution.py
+++ b/solution.py
@@ -263,6 +263,7 @@
     @pl.when(first)
     def _():
         each(step_four, 0, 2)
+        each(step_one, 2, total)
         each(step_five, 0, 2)
 
     @pl.when(jnp.logical_not(has_right))
@@ -314,13 +315,13 @@
 
         products(one, 0, 2, rows)
 
+        @pl.when(lends_late)
+        def _():
+            late_left(part).start()
+
         @pl.when(has_right)
         def _():
             block_right(part).start()
-
-        @pl.when(lends_late)
-        def _():
-            late_left(part).start()
 
     each(first_stage, 0, PARTS)
 
@@ -329,7 +330,7 @@
         for part in range(PARTS):
             early_left(part).start()
 
-        for step in (step_one, step_two, step_three, step_four, step_five):
+        for step in (step_two, step_three, step_four, step_five):
             each(step, 2, total)
 
         def second_stage(part):

time: 63.1 us -> 62.3 us (0.987)
  no operation moved by 1% of the time
where the time goes in v4:
time: 62.3 us; the launch traced here: 62.1 us
  Pallas kernels  60.4 us (97%)
  local copies, waits for them, and re-layouts  1.67 us (3%)
    pallas_call x1, Pallas kernels, on_device(): pl.pallas_call(functools.partial(kernel, lax.axis_size('col')), out_shape...  60.4 us
    unnamed x1, local copies, waits for them, and re-layouts  1.67 us

profile of v4, /device:TPU:44, one launch (start us, length us, event | category | flops | bytes accessed | tf_op | source)
XLA Modules:
  0.0 62.1 jit_solution(1722967541548337280)
XLA Ops:
  0.0 60.4 %shard_map.37 = f32[128,512]{1,0:T(8,128)} custom-call(f32[128,512]{1,0:T(8,128)} %vec.1, f32[1,4,32,512]{3,2,1,0:T(8,128)} %fac.1, s32[32]{0:T(128)} %off.1), custom_call_target="tpu_custom_call" | custom-call | tf_op jit(solution)/shard_map/pallas_call | solution.py:419
  60.4 1.7 %copy.5 = f32[128,512]{1,0:T(8,128)} copy(f32[128,512]{1,0:T(8,128)} %shard_map.37) | data formatting | bytes 524288
